TPU v7x, 256 devices: a whole 4x4x8 slice. The times are simulated.
256 devices in a mesh: row: 8 (over x, core), col: 32 (over z, y).
Axes of the slice: x: 4, y: 4, z: 8, core: 2. Of those that a mesh axis runs over, the one named last changes fastest.
Arguments:
- ancestor_order: int32 [2, 48], replicated, may hold values from 0 to 47, each once within a row
- factor_rows: bfloat16 [2, 24576, 512], P(None, ('row', 'col')), may hold values from -0.0390625 to 0.0390625
- factor_inverse: bfloat16 [2, 512, 512], replicated
- ancestor_inverse: bfloat16 [24576, 24576], P('col', 'row'), may hold values from -6 to 6
- diagonal_inverse: float32 [2, 512, 512], P(None, None, 'row'), may hold values from -6 to 6
Outputs:
- offdiag_inverse: bfloat16 [2, 24576, 512], P(None, 'col', 'row')
- diag_updated: float32 [2, 512, 512], P(None, None, 'row')
Inputs may be any that keep to these rules, and one draw needn't show every extreme that they name: `ancestor_order`: each row lists every ancestor block once; its first 40 entries are the blocks coupled to that supernode.
All inputs are finite; a program needn't handle non-finite values.
Results may differ from a plain program's by a relative error of at most 0.011.
Values may be sent and summed in bfloat16 or wider, within the bound.
No kernel may reach another device: no remote copies, remote signals or barrier semaphores. Data moves between devices by JAX's collectives and lax.ppermute only.
A program may use at most 128 MiB of HBM per device.

v0:
```python
import jax
import jax.numpy as jnp
from jax import lax
from jax.sharding import Mesh
from jax.sharding import PartitionSpec as P

NSEL = 40
XS, CORES, ZS, YS = (4, 2, 8, 4)
ROW = ("x", "core")
COL = ("z", "y")
ALL = ("x", "core", "z", "y")
F32 = jnp.float32
BF16 = jnp.bfloat16


def shift(array, axis, size, by):
    return lax.ppermute(array, axis, [(i, (i + by) % size) for i in range(size)])


def direct_ring(array, axis, size):
    return [array] + [
        shift(array, axis, size, d if d <= size // 2 else d - size) for d in range(1, size)
    ]


def relay_ring(array, axis, size, halved):
    got = [array] + [None] * (size - 1)
    right = left = array
    for step in range(1, size // 2):
        right = shift(right, axis, size, 1)
        left = shift(left, axis, size, -1)
        got[step], got[size - step] = (right, left)
    if halved:
        half = array.shape[0] // 2
        got[size // 2] = jnp.concatenate(
            [shift(right[:half], axis, size, 1), shift(left[half:], axis, size, -1)], axis=0
        )
    else:
        got[size // 2] = shift(right, axis, size, 1)
    return got


def placed_by_owner(got, own, axis):
    size, width = (len(got), got[0].shape[axis])
    dims = list(got[0].shape)
    dims[axis] *= size
    whole = jnp.zeros(dims, got[0].dtype)
    for d, chunk in enumerate(got):
        whole = lax.dynamic_update_slice_in_dim(whole, chunk, (own - d) % size * width, axis)
    return whole


def panel_y_then_z(piece):
    part = placed_by_owner(direct_ring(piece, "y", YS), lax.axis_index("y"), 0)
    return lax.all_gather(part, "z", axis=0, tiled=True)


def near_z_then_y(piece):
    part = placed_by_owner(relay_ring(piece[None], "z", ZS, False), lax.axis_index("z"), 0)[:, None]
    return [part, shift(part, "y", YS, 1), shift(part, "y", YS, -1)]


def far_chunk(near):
    half = near[0].shape[0] // 2
    right = shift(near[1][:half], "y", YS, 1)
    return jnp.concatenate([right, shift(near[2][half:], "y", YS, -1)], axis=0)


def device(x, core, z, y):
    return ((x * CORES + core) * ZS + z) * YS + y


def root_of(z):
    return (z // CORES, z % CORES)


def from_root(array, target):
    pairs = []
    for z in range(ZS):
        for y in range(YS):
            x, core = root_of(z)
            pairs.append((device(x, core, z, y), device(*target(x, core, z, y))))
    return lax.ppermute(array, ALL, pairs)


def along_x(slab, core, shifts):
    return sum((from_root(slab, lambda x, c, z, y: ((x + by) % XS, core, z, y)) for by in shifts))


def pair_sum(partial):
    first = lax.axis_index("core") == 0
    given = lax.ppermute(jnp.where(first, partial[1], partial[0]), "core", [(0, 1), (1, 0)])
    pair = jnp.where(first, partial[0], partial[1]).astype(F32) + given.astype(F32)
    return pair.astype(BF16)


def sum_over_x(pair):
    x = lax.axis_index("x")
    pair = pair.reshape(XS, -1, pair.shape[1])
    tile = lambda k: lax.dynamic_index_in_dim(pair, (x + k) % XS, 0, keepdims=False)
    opposite = shift(tile(2), "x", XS, 2)
    near = shift(tile(1), "x", XS, 1).astype(F32) + shift(tile(3), "x", XS, -1).astype(F32)
    return tile(0).astype(F32) + opposite.astype(F32) + near


def exchanged(array, axis, size, by):
    return lax.ppermute(array, axis, [(i, i ^ by) for i in range(size)])


def summed_over_col(array):
    y = lax.axis_index("y")
    quarters = array.reshape(YS, -1, array.shape[1])
    own = lambda k: lax.dynamic_index_in_dim(quarters, y ^ k, 0, keepdims=False)
    part = own(0).astype(F32)
    for k in range(1, YS):
        part = part + exchanged(own(k), "y", YS, k).astype(F32)
    part = lax.optimization_barrier(part.astype(BF16))
    copies = jnp.broadcast_to(part[None], (ZS, *part.shape))
    part = lax.all_to_all(copies, "z", split_axis=0, concat_axis=0, tiled=True)
    part = lax.optimization_barrier(part.astype(F32).sum(axis=0).astype(BF16))
    whole = jnp.zeros(quarters.shape, BF16)
    for k in range(YS):
        got = part if k == 0 else exchanged(part, "y", YS, k)
        whole = lax.dynamic_update_slice_in_dim(whole, got[None], y ^ k, 0)
    return whole.reshape(array.shape)


def own_slab_of_both(array):
    core = lax.axis_index("core")
    slabs = array.reshape(CORES, -1, array.shape[1])
    kept = lax.dynamic_index_in_dim(slabs, core, 0, keepdims=False)
    given = lax.dynamic_index_in_dim(slabs, 1 - core, 0, keepdims=False)
    got = lax.ppermute(given, "core", [(0, 1), (1, 0)])
    return jnp.stack([jnp.where(core == 0, kept, got), jnp.where(core == 0, got, kept)])


def body(listing, pieces, factor_inv, inverse_block, diag_inv):
    piece_rows, width = pieces.shape[1:]
    row = lax.axis_index(ROW)
    col = lax.axis_index(COL)
    core, z, y = (lax.axis_index("core"), lax.axis_index("z"), lax.axis_index("y"))
    chosen = listing[:, :NSEL]

    def keep_of(first, count):
        labels = (first + jnp.arange(count, dtype=jnp.int32)) // width
        return jnp.any(chosen[:, :, None] == labels[None, None, :], axis=1).astype(F32)

    own_keep = keep_of((row * ZS * YS + col) * piece_rows, piece_rows)
    normed = jnp.einsum("srk,skj->srj", pieces, factor_inv, preferred_element_type=F32)
    normed = (normed * own_keep[:, :, None]).astype(BF16)
    rows = inverse_block.shape[0]

    def partial_of(panel):
        return jnp.einsum("qj,pq->jp", panel, inverse_block, preferred_element_type=F32).astype(
            BF16
        )

    first = core == 0
    near = near_z_then_y(normed[1])
    deep = rows // (piece_rows * YS)
    of_slab = lambda part, lane: lax.dynamic_slice_in_dim(part, lane * deep, deep, 0)
    far_part = from_root(of_slab(near[0], (y + 2) % YS), lambda x, c, z, y: (x, c, z, (y + 2) % YS))
    slab_parts = [of_slab(near[0], y), of_slab(near[1], y), far_part, of_slab(near[2], y)]
    slab_1 = placed_by_owner(slab_parts, y, 1).reshape(rows, width)
    sent_1 = along_x(slab_1, 1, (1, -1, -2))
    panel_0 = panel_y_then_z(normed[0])
    panel_0, near = lax.optimization_barrier((panel_0, near))
    chunks = [near[0], near[1], far_chunk(near), near[2]]
    slab_0 = lax.dynamic_slice_in_dim(panel_0, y * rows, rows, 0)
    sent_0 = along_x(slab_0, 0, (1, -1, 2))
    partial = [partial_of(panel_0)]
    chunks, partial[0] = lax.optimization_barrier((chunks, partial[0]))
    across = from_root(jnp.where(first, slab_1, slab_0), lambda x, c, z, y: (x, 1 - c, z, y))
    partial.append(partial_of(placed_by_owner(chunks, y, 1).reshape(panel_0.shape)))
    home = row == z
    factor_slab = jnp.where(home, jnp.where(first, slab_0, slab_1), sent_0 + sent_1 + across)
    pair, factor_slab = lax.optimization_barrier((pair_sum(partial), factor_slab))
    product = sum_over_x(pair)
    col_keep = lax.dynamic_index_in_dim(keep_of(col * rows, rows), core, 0)
    offdiag = lax.optimization_barrier((-(product * col_keep)).astype(BF16))
    term = -jnp.dot(offdiag, factor_slab, preferred_element_type=F32)
    correction = own_slab_of_both(summed_over_col(term.astype(BF16)))
    return (
        own_slab_of_both(offdiag).transpose(0, 2, 1),
        diag_inv + correction.astype(F32).transpose(0, 2, 1),
    )


def solution(mesh):
    torus = Mesh(mesh.devices.reshape(XS, CORES, ZS, YS), ALL)
    return jax.shard_map(
        body,
        mesh=torus,
        in_specs=(P(), P(None, ALL, None), P(), P(COL, ROW), P(None, None, ROW)),
        out_specs=(P(None, COL, ROW), P(None, None, ROW)),
        check_vma=False,
    )
```

profile of v0, /device:TPU:1, one launch (start us, length us, event | category | flops | bytes accessed | tf_op | source)
XLA Modules:
  0.0 166.6 jit_solution(9911630012255583256)
XLA Ops:
  9.7 3.8 %collective-permute-start.1 = (bf16[96,512]{1,0:T(8,128)(2,1)S(1)}, bf16[96,512]{1,0:T(8,128)(2,1)S(1)}, u32[]{:S(2)}, u32[]{:S(2)}) collective-permute-start(bf16[96,512]{1,0:T(8,128)(2,1)S(1)} %get-tuple-element.36), channel_id=1, source_target_pairs={{0,2},{1,3},{2,0},{3,1},{4,6},{5,7},{6,4},{7,5},{8,10},{9,11},{10,... | collective-permute-start | bytes 294920 | tf_op jit(solution)/shard_map/ppermute | solution.py:17
  13.9 2.3 %collective-permute-start.2 = (bf16[96,512]{1,0:T(8,128)(2,1)S(1)}, bf16[96,512]{1,0:T(8,128)(2,1)S(1)}, u32[]{:S(2)}, u32[]{:S(2)}) collective-permute-start(bf16[96,512]{1,0:T(8,128)(2,1)S(1)} %get-tuple-element.36), channel_id=1, source_target_pairs={{0,3},{1,0},{2,1},{3,2},{4,7},{5,4},{6,5},{7,6},{8,11},{9,8},{10,9... | collective-permute-start | bytes 294920 | tf_op jit(solution)/shard_map/ppermute | solution.py:17
  16.3 3.8 %collective-permute-done = bf16[96,512]{1,0:T(8,128)(2,1)S(1)} collective-permute-done((bf16[96,512]{1,0:T(8,128)(2,1)S(1)}, bf16[96,512]{1,0:T(8,128)(2,1)S(1)}, u32[]{:S(2)}, u32[]{:S(2)}) %collective-permute-start) | collective-permute-done | bytes 98336 | tf_op jit(solution)/shard_map/ppermute | solution.py:17
  21.1 3.8 %collective-permute-start.7 = (bf16[1,96,512]{2,1,0:T(8,128)(2,1)S(1)}, bf16[1,96,512]{2,1,0:T(8,128)(2,1)S(1)}, u32[]{:S(2)}, u32[]{:S(2)}) collective-permute-start(bf16[1,96,512]{2,1,0:T(8,128)(2,1)S(1)} %get-tuple-element.35), channel_id=1, source_target_pairs={{0,28},{4,0},{8,4},{12,8},{16,12},{20,16},{24,20},{28,24},{1,29},{... | collective-permute-start | bytes 294920 | tf_op jit(solution)/shard_map/ppermute | solution.py:17
  26.8 2.8 %collective-permute-start.8 = (bf16[1,96,512]{2,1,0:T(8,128)(2,1)S(1)}, bf16[1,96,512]{2,1,0:T(8,128)(2,1)S(1)}, u32[]{:S(2)}, u32[]{:S(2)}) collective-permute-start(bf16[1,96,512]{2,1,0:T(8,128)(2,1)S(1)} %collective-permute-done.7), channel_id=1, source_target_pairs={{0,28},{4,0},{8,4},{12,8},{16,12},{20,16},{24,20},{28,24},{1,29},{... | collective-permute-start | bytes 294920 | tf_op jit(solution)/shard_map/ppermute | solution.py:17
  31.5 2.8 %collective-permute-start.9 = (bf16[1,96,512]{2,1,0:T(8,128)(2,1)S(1)}, bf16[1,96,512]{2,1,0:T(8,128)(2,1)S(1)}, u32[]{:S(2)}, u32[]{:S(2)}) collective-permute-start(bf16[1,96,512]{2,1,0:T(8,128)(2,1)S(1)} %collective-permute-done.8), channel_id=1, source_target_pairs={{0,28},{4,0},{8,4},{12,8},{16,12},{20,16},{24,20},{28,24},{1,29},{... | collective-permute-start | bytes 294920 | tf_op jit(solution)/shard_map/ppermute | solution.py:17
  36.2 7.8 %collective-permute-done.6 = bf16[1,96,512]{2,1,0:T(8,128)(2,1)S(1)} collective-permute-done((bf16[1,96,512]{2,1,0:T(8,128)(2,1)S(1)}, bf16[1,96,512]{2,1,0:T(8,128)(2,1)S(1)}, u32[]{:S(2)}, u32[]{:S(2)}) %collective-permute-start.6) | collective-permute-done | bytes 98336 | tf_op jit(solution)/shard_map/ppermute | solution.py:17
  49.3 7.6 %collective-permute-done.10 = bf16[8,1,96,512]{3,2,1,0:T(8,128)(2,1)} collective-permute-done((bf16[8,1,96,512]{3,2,1,0:T(8,128)(2,1)S(1)}, bf16[8,1,96,512]{3,2,1,0:T(8,128)(2,1)}, u32[]{:S(2)}, u32[]{:S(2)}) %collective-permute-start.10) | collective-permute-done | bytes 786464 | tf_op jit(solution)/shard_map/ppermute | solution.py:17
  63.6 8.1 %all-gather.2.cloned.1.call-done = bf16[3072,512]{1,0:T(8,128)(2,1)} async-done(((bf16[384,512]{1,0:T(8,128)(2,1)}), bf16[3072,512]{1,0:T(8,128)(2,1)}) %all-gather.2.cloned.1.call-update) | async-done | bytes 3145744 | tf_op jit(solution)/shard_map/all_gather | solution.py:55
  72.8 2.3 %collective-permute-start.13 = (bf16[4,1,96,512]{3,2,1,0:T(8,128)(2,1)S(1)}, bf16[4,1,96,512]{3,2,1,0:T(8,128)(2,1)S(1)}, u32[]{:S(2)}, u32[]{:S(2)}) collective-permute-start(bf16[4,1,96,512]{3,2,1,0:T(8,128)(2,1)S(1)} %slice.19), channel_id=1, source_target_pairs={{0,3},{1,0},{2,1},{3,2},{4,7},{5,4},{6,5},{7,6},{8,11},{9,8},{10,9... | collective-permute-start | bytes 1179656 | tf_op jit(solution)/shard_map/ppermute | solution.py:17
  75.1 5.9 %convolution_convert_fusion.1 = bf16[512,768]{1,0:T(8,128)(2,1)S(1)} fusion(bf16[3072,512]{1,0:T(8,128)(2,1)} %all-gather.2.cloned.1.call-done, bf16[768,3072]{1,0:T(8,128)(2,1)} %param.8), kind=kOutput, calls=%fused_computation.2 | convolution fusion | flops 2416312320 | bytes 8650752 | tf_op jit(solution)/shard_map/qj,pq->jp/dot_general | solution.py:154
  81.1 2.6 %broadcast_select_fusion = (bf16[768,512]{1,0:T(8,128)(2,1)}, bf16[768,512]{1,0:T(8,128)(2,1)S(1)}) fusion(pred[]{:T(512)S(6)} %eq.63, bf16[2,4,96,512]{3,2,1,0:T(8,128)(2,1)S(1)} %dynamic-slice_dynamic-update-slice_fusion, bf16[3072,512]{1,0:T(8,128)(2,1)} %all-gather.2.cloned.1.call-done, s32[]{:T(128)S(6)} %select_n.299), kind=kLoop, calls=%fused_computation.9 | loop fusion | flops 393216 | bytes 3145733 | tf_op jit(solution)/shard_map/jit(_where)/select_n | solution.py:173
  91.7 3.8 %broadcast_select_fusion.1 = (bf16[512,768]{1,0:T(8,128)(2,1)}, bf16[512,768]{1,0:T(8,128)(2,1)}) fusion(bf16[512,768]{1,0:T(8,128)(2,1)S(1)} %convolution_convert_fusion.1, pred[]{:T(512)S(6)} %eq.63, bf16[3072,512]{1,0:T(8,128)(2,1)S(1)} %bitcast.96, bf16[768,3072]{1,0:T(8,128)(2,1)S(1)} %bitcast.108), kind=kOutput, calls=%fused_computation.10 | convolution fusion | flops 2416705536 | bytes 10223617 | tf_op jit(solution)/shard_map/qj,pq->jp/dot_general | solution.py:154
  95.5 7.2 %collective-permute-start.14 = (bf16[512,768]{1,0:T(8,128)(2,1)}, bf16[512,768]{1,0:T(8,128)(2,1)}, u32[]{:S(2)}, u32[]{:S(2)}) collective-permute-start(bf16[512,768]{1,0:T(8,128)(2,1)} %get-tuple-element.40), channel_id=1, source_target_pairs={{0,32},{32,0},{1,33},{33,1},{2,34},{34,2},{3,35},{35,3},{4,36},{36... | collective-permute-start | bytes 2359304 | tf_op jit(solution)/shard_map/ppermute | solution.py:92
  102.7 2.7 %add_select_fusion = bf16[768,512]{1,0:T(8,128)(2,1)S(1)} fusion(bf16[768,512]{1,0:T(8,128)(2,1)S(1)} %collective-permute-done.22, bf16[768,512]{1,0:T(8,128)(2,1)} %collective-permute-done.21, bf16[768,512]{1,0:T(8,128)(2,1)} %collective-permute-done.19, bf16[768,512]{1,0:T(8,128)(2,1)} %collective-permute-done.20, ...), kind=kLoop, calls=%fused_computation.8 | loop fusion | flops 3145728 | bytes 7864322 | tf_op jit(solution)/shard_map/jit(_where)/select_n | solution.py:176
  108.8 4.4 %collective-permute-done.23 = bf16[128,768]{1,0:T(8,128)(2,1)S(1)} collective-permute-done((bf16[128,768]{1,0:T(8,128)(2,1)S(1)}, bf16[128,768]{1,0:T(8,128)(2,1)S(1)}, u32[]{:S(2)}, u32[]{:S(2)}) %collective-permute-start.23) | collective-permute-done | bytes 196640 | tf_op jit(solution)/shard_map/ppermute | solution.py:17
  113.2 2.0 %collective-permute-done.24 = bf16[128,768]{1,0:T(8,128)(2,1)S(1)} collective-permute-done((bf16[128,768]{1,0:T(8,128)(2,1)S(1)}, bf16[128,768]{1,0:T(8,128)(2,1)S(1)}, u32[]{:S(2)}, u32[]{:S(2)}) %collective-permute-start.24) | collective-permute-done | bytes 196640 | tf_op jit(solution)/shard_map/ppermute | solution.py:17
  120.5 2.1 %collective-permute-done.28 = bf16[32,512]{1,0:T(8,128)(2,1)S(1)} collective-permute-done((bf16[32,512]{1,0:T(8,128)(2,1)S(1)}, bf16[32,512]{1,0:T(8,128)(2,1)S(1)}, u32[]{:S(2)}, u32[]{:S(2)}) %collective-permute-start.28) | collective-permute-done | bytes 32800 | tf_op jit(solution)/shard_map/ppermute | solution.py:107
  123.4 11.4 %all-to-all-start = ((bf16[8,32,512]{2,1,0:T(8,128)(2,1)}), bf16[8,32,512]{2,1,0:T(8,128)(2,1)S(1)}, u32[]{:S(2)}, u32[]{:S(2)}) async-start(bf16[8,32,512]{2,1,0:T(8,128)(2,1)} %broadcast_in_dim.68), calls=%async_computation | async-start | bytes 524288 | tf_op jit(solution)/shard_map/all_to_all | solution.py:119
  134.8 4.1 %collective-permute-start.26 = (bf16[64,768]{1,0:T(8,128)(2,1)S(1)}, bf16[64,768]{1,0:T(8,128)(2,1)S(1)}, u32[]{:S(2)}, u32[]{:S(2)}) collective-permute-start(bf16[64,768]{1,0:T(8,128)(2,1)S(1)} %dynamic-slice_bitcast_fusion.3), channel_id=1, source_target_pairs={{0,32},{32,0},{1,33},{33,1},{2,34},{34,2},{3,35},{35,3},{4,36},{36... | collective-permute-start | bytes 294920 | tf_op jit(solution)/shard_map/ppermute | solution.py:133
  139.8 4.3 %all-to-all-done = bf16[8,32,512]{2,1,0:T(8,128)(2,1)S(1)} async-done(((bf16[8,32,512]{2,1,0:T(8,128)(2,1)}), bf16[8,32,512]{2,1,0:T(8,128)(2,1)S(1)}, u32[]{:S(2)}, u32[]{:S(2)}) %all-to-all-start) | async-done | bytes 262176 | tf_op jit(solution)/shard_map/all_to_all | solution.py:119
  144.5 2.2 %collective-permute-start.31 = (bf16[32,512]{1,0:T(8,128)(2,1)S(1)}, bf16[32,512]{1,0:T(8,128)(2,1)S(1)}, u32[]{:S(2)}, u32[]{:S(2)}) collective-permute-start(bf16[32,512]{1,0:T(8,128)(2,1)S(1)} %reduce_sum.12), channel_id=1, source_target_pairs={{0,2},{1,3},{2,0},{3,1},{4,6},{5,7},{6,4},{7,5},{8,10},{9,11},{10,... | collective-permute-start | bytes 98312 | tf_op jit(solution)/shard_map/ppermute | solution.py:107
  147.6 1.9 %collective-permute-done.30 = bf16[32,512]{1,0:T(8,128)(2,1)S(1)} collective-permute-done((bf16[32,512]{1,0:T(8,128)(2,1)S(1)}, bf16[32,512]{1,0:T(8,128)(2,1)S(1)}, u32[]{:S(2)}, u32[]{:S(2)}) %collective-permute-start.30) | collective-permute-done | bytes 32800 | tf_op jit(solution)/shard_map/ppermute | solution.py:107
  149.6 8.5 %collective-permute-start.33 = (bf16[64,512]{1,0:T(8,128)(2,1)S(1)}, bf16[64,512]{1,0:T(8,128)(2,1)S(1)}, u32[]{:S(2)}, u32[]{:S(2)}) collective-permute-start(bf16[64,512]{1,0:T(8,128)(2,1)S(1)} %dynamic-slice_bitcast_fusion.4), channel_id=1, source_target_pairs={{0,32},{32,0},{1,33},{33,1},{2,34},{34,2},{3,35},{35,3},{4,36},{36... | collective-permute-start | bytes 196616 | tf_op jit(solution)/shard_map/ppermute | solution.py:133
  (130 shorter events, 43.4 us)
Async XLA Ops:
  7.2 64.5 %all-gather.2.cloned.1.call-start = ((), (), s32[]{:S(2)}) async-start(), calls=%async_computation.1 | async-start | bytes 3538944 | tf_op jit(solution)/shard_map/all_gather | solution.py:55
  9.7 10.5 %collective-permute-start.1 = (bf16[96,512]{1,0:T(8,128)(2,1)S(1)}, bf16[96,512]{1,0:T(8,128)(2,1)S(1)}, u32[]{:S(2)}, u32[]{:S(2)}) collective-permute-start(bf16[96,512]{1,0:T(8,128)(2,1)S(1)} %get-tuple-element.36), channel_id=1, source_target_pairs={{0,2},{1,3},{2,0},{3,1},{4,6},{5,7},{6,4},{7,5},{8,10},{9,11},{10,... | collective-permute-start | bytes 294920 | tf_op jit(solution)/shard_map/ppermute | solution.py:17
  13.5 6.6 %collective-permute-start = (bf16[96,512]{1,0:T(8,128)(2,1)S(1)}, bf16[96,512]{1,0:T(8,128)(2,1)S(1)}, u32[]{:S(2)}, u32[]{:S(2)}) collective-permute-start(bf16[96,512]{1,0:T(8,128)(2,1)S(1)} %get-tuple-element.36), channel_id=1, source_target_pairs={{0,1},{1,2},{2,3},{3,0},{4,5},{5,6},{6,7},{7,4},{8,9},{9,10},{10,1... | collective-permute-start | bytes 294920 | tf_op jit(solution)/shard_map/ppermute | solution.py:17
  13.9 6.3 %collective-permute-start.2 = (bf16[96,512]{1,0:T(8,128)(2,1)S(1)}, bf16[96,512]{1,0:T(8,128)(2,1)S(1)}, u32[]{:S(2)}, u32[]{:S(2)}) collective-permute-start(bf16[96,512]{1,0:T(8,128)(2,1)S(1)} %get-tuple-element.36), channel_id=1, source_target_pairs={{0,3},{1,0},{2,1},{3,2},{4,7},{5,4},{6,5},{7,6},{8,11},{9,8},{10,9... | collective-permute-start | bytes 294920 | tf_op jit(solution)/shard_map/ppermute | solution.py:17
  31.5 12.6 %collective-permute-start.9 = (bf16[1,96,512]{2,1,0:T(8,128)(2,1)S(1)}, bf16[1,96,512]{2,1,0:T(8,128)(2,1)S(1)}, u32[]{:S(2)}, u32[]{:S(2)}) collective-permute-start(bf16[1,96,512]{2,1,0:T(8,128)(2,1)S(1)} %collective-permute-done.8), channel_id=1, source_target_pairs={{0,28},{4,0},{8,4},{12,8},{16,12},{20,16},{24,20},{28,24},{1,29},{... | collective-permute-start | bytes 294920 | tf_op jit(solution)/shard_map/ppermute | solution.py:17
  36.2 7.9 %collective-permute-start.6 = (bf16[1,96,512]{2,1,0:T(8,128)(2,1)S(1)}, bf16[1,96,512]{2,1,0:T(8,128)(2,1)S(1)}, u32[]{:S(2)}, u32[]{:S(2)}) collective-permute-start(bf16[1,96,512]{2,1,0:T(8,128)(2,1)S(1)} %collective-permute-done.5), channel_id=1, source_target_pairs={{0,4},{4,8},{8,12},{12,16},{16,20},{20,24},{24,28},{28,0},{1,5},{5... | collective-permute-start | bytes 294920 | tf_op jit(solution)/shard_map/ppermute | solution.py:17
  44.1 12.7 %collective-permute-start.10 = (bf16[8,1,96,512]{3,2,1,0:T(8,128)(2,1)S(1)}, bf16[8,1,96,512]{3,2,1,0:T(8,128)(2,1)}, u32[]{:S(2)}, u32[]{:S(2)}) collective-permute-start(bf16[8,1,96,512]{3,2,1,0:T(8,128)(2,1)S(1)} %bitcast_dynamic-update-slice_fusion), channel_id=1, source_target_pairs={{0,1},{1,2},{2,3},{3,0},{4,5},{5,6},{6,7},{7,4},{8,9},{9,10},{10,1... | collective-permute-start | bytes 2359304 | tf_op jit(solution)/shard_map/ppermute | solution.py:17
  46.0 12.8 %collective-permute-start.11 = (bf16[8,1,96,512]{3,2,1,0:T(8,128)(2,1)S(1)}, bf16[8,1,96,512]{3,2,1,0:T(8,128)(2,1)S(1)}, u32[]{:S(2)}, u32[]{:S(2)}) collective-permute-start(bf16[8,1,96,512]{3,2,1,0:T(8,128)(2,1)S(1)} %bitcast_dynamic-update-slice_fusion), channel_id=1, source_target_pairs={{0,3},{1,0},{2,1},{3,2},{4,7},{5,4},{6,5},{7,6},{8,11},{9,8},{10,9... | collective-permute-start | bytes 2359304 | tf_op jit(solution)/shard_map/ppermute | solution.py:17
  47.9 9.9 %collective-permute-start.15 = (bf16[2,1,96,512]{3,2,1,0:T(8,128)(2,1)}, bf16[2,1,96,512]{3,2,1,0:T(8,128)(2,1)}, u32[]{:S(2)}, u32[]{:S(2)}) collective-permute-start(bf16[2,1,96,512]{3,2,1,0:T(8,128)(2,1)} %get-tuple-element.29), channel_id=1, source_target_pairs={{0,2},{1,3},{2,0},{3,1},{36,38},{37,39},{38,36},{39,37},{72,74},{7... | collective-permute-start | bytes 589832 | tf_op jit(solution)/shard_map/ppermute | solution.py:83
  58.9 29.9 %collective-permute-start.20 = (bf16[768,512]{1,0:T(8,128)(2,1)S(1)}, bf16[768,512]{1,0:T(8,128)(2,1)}, u32[]{:S(2)}, u32[]{:S(2)}) collective-permute-start(bf16[768,512]{1,0:T(8,128)(2,1)S(1)} %bitcast.93), channel_id=1, source_target_pairs={{0,224},{1,225},{2,226},{3,227},{36,228},{37,229},{38,230},{39,231... | collective-permute-start | bytes 2359304 | tf_op jit(solution)/shard_map/ppermute | solution.py:83
  60.4 30.0 %collective-permute-start.19 = (bf16[768,512]{1,0:T(8,128)(2,1)S(1)}, bf16[768,512]{1,0:T(8,128)(2,1)}, u32[]{:S(2)}, u32[]{:S(2)}) collective-permute-start(bf16[768,512]{1,0:T(8,128)(2,1)S(1)} %bitcast.94), channel_id=1, source_target_pairs={{0,96},{1,97},{2,98},{3,99},{36,100},{37,101},{38,102},{39,103},{7... | collective-permute-start | bytes 2359304 | tf_op jit(solution)/shard_map/ppermute | solution.py:83
  62.0 33.5 %collective-permute-start.21 = (bf16[768,512]{1,0:T(8,128)(2,1)S(1)}, bf16[768,512]{1,0:T(8,128)(2,1)}, u32[]{:S(2)}, u32[]{:S(2)}) collective-permute-start(bf16[768,512]{1,0:T(8,128)(2,1)S(1)} %bitcast.95), channel_id=1, source_target_pairs={{0,160},{1,161},{2,162},{3,163},{36,164},{37,165},{38,166},{39,167... | collective-permute-start | bytes 2359304 | tf_op jit(solution)/shard_map/ppermute | solution.py:83
  72.8 10.9 %collective-permute-start.13 = (bf16[4,1,96,512]{3,2,1,0:T(8,128)(2,1)S(1)}, bf16[4,1,96,512]{3,2,1,0:T(8,128)(2,1)S(1)}, u32[]{:S(2)}, u32[]{:S(2)}) collective-permute-start(bf16[4,1,96,512]{3,2,1,0:T(8,128)(2,1)S(1)} %slice.19), channel_id=1, source_target_pairs={{0,3},{1,0},{2,1},{3,2},{4,7},{5,4},{6,5},{7,6},{8,11},{9,8},{10,9... | collective-permute-start | bytes 1179656 | tf_op jit(solution)/shard_map/ppermute | solution.py:17
  75.1 10.2 %collective-permute-start.12 = (bf16[4,1,96,512]{3,2,1,0:T(8,128)(2,1)S(1)}, bf16[4,1,96,512]{3,2,1,0:T(8,128)(2,1)S(1)}, u32[]{:S(2)}, u32[]{:S(2)}) collective-permute-start(bf16[4,1,96,512]{3,2,1,0:T(8,128)(2,1)S(1)} %slice.18), channel_id=1, source_target_pairs={{0,1},{1,2},{2,3},{3,0},{4,5},{5,6},{6,7},{7,4},{8,9},{9,10},{10,1... | collective-permute-start | bytes 1179656 | tf_op jit(solution)/shard_map/ppermute | solution.py:17
  83.7 19.0 %collective-permute-start.18 = (bf16[768,512]{1,0:T(8,128)(2,1)S(1)}, bf16[768,512]{1,0:T(8,128)(2,1)}, u32[]{:S(2)}, u32[]{:S(2)}) collective-permute-start(bf16[768,512]{1,0:T(8,128)(2,1)S(1)} %get-tuple-element.25), channel_id=1, source_target_pairs={{0,128},{1,129},{2,130},{3,131},{36,132},{37,133},{38,134},{39,135... | collective-permute-start | bytes 2359304 | tf_op jit(solution)/shard_map/ppermute | solution.py:83
  85.3 17.5 %collective-permute-start.17 = (bf16[768,512]{1,0:T(8,128)(2,1)S(1)}, bf16[768,512]{1,0:T(8,128)(2,1)}, u32[]{:S(2)}, u32[]{:S(2)}) collective-permute-start(bf16[768,512]{1,0:T(8,128)(2,1)S(1)} %get-tuple-element.25), channel_id=1, source_target_pairs={{0,192},{1,193},{2,194},{3,195},{36,196},{37,197},{38,198},{39,199... | collective-permute-start | bytes 2359304 | tf_op jit(solution)/shard_map/ppermute | solution.py:83
  88.8 14.0 %collective-permute-start.16 = (bf16[768,512]{1,0:T(8,128)(2,1)S(1)}, bf16[768,512]{1,0:T(8,128)(2,1)}, u32[]{:S(2)}, u32[]{:S(2)}) collective-permute-start(bf16[768,512]{1,0:T(8,128)(2,1)S(1)} %get-tuple-element.25), channel_id=1, source_target_pairs={{0,64},{1,65},{2,66},{3,67},{36,68},{37,69},{38,70},{39,71},{72,13... | collective-permute-start | bytes 2359304 | tf_op jit(solution)/shard_map/ppermute | solution.py:83
  90.4 12.3 %collective-permute-start.22 = (bf16[768,512]{1,0:T(8,128)(2,1)}, bf16[768,512]{1,0:T(8,128)(2,1)S(1)}, u32[]{:S(2)}, u32[]{:S(2)}) collective-permute-start(bf16[768,512]{1,0:T(8,128)(2,1)} %get-tuple-element.24), channel_id=1, source_target_pairs={{0,32},{1,33},{2,34},{3,35},{36,4},{37,5},{38,6},{39,7},{72,104},{... | collective-permute-start | bytes 2359304 | tf_op jit(solution)/shard_map/ppermute | solution.py:83
  95.5 10.0 %collective-permute-start.14 = (bf16[512,768]{1,0:T(8,128)(2,1)}, bf16[512,768]{1,0:T(8,128)(2,1)}, u32[]{:S(2)}, u32[]{:S(2)}) collective-permute-start(bf16[512,768]{1,0:T(8,128)(2,1)} %get-tuple-element.40), channel_id=1, source_target_pairs={{0,32},{32,0},{1,33},{33,1},{2,34},{34,2},{3,35},{35,3},{4,36},{36... | collective-permute-start | bytes 2359304 | tf_op jit(solution)/shard_map/ppermute | solution.py:92
  107.0 6.2 %collective-permute-start.23 = (bf16[128,768]{1,0:T(8,128)(2,1)S(1)}, bf16[128,768]{1,0:T(8,128)(2,1)S(1)}, u32[]{:S(2)}, u32[]{:S(2)}) collective-permute-start(bf16[128,768]{1,0:T(8,128)(2,1)S(1)} %get-tuple-element.26), channel_id=1, source_target_pairs={{0,128},{64,192},{128,0},{192,64},{1,129},{65,193},{129,1},{193,65... | collective-permute-start | bytes 589832 | tf_op jit(solution)/shard_map/ppermute | solution.py:17
  107.1 6.1 %collective-permute-start.25 = (bf16[128,768]{1,0:T(8,128)(2,1)S(1)}, bf16[128,768]{1,0:T(8,128)(2,1)S(1)}, u32[]{:S(2)}, u32[]{:S(2)}) collective-permute-start(bf16[128,768]{1,0:T(8,128)(2,1)S(1)} %get-tuple-element.27), channel_id=1, source_target_pairs={{0,192},{64,0},{128,64},{192,128},{1,193},{65,1},{129,65},{193,129... | collective-permute-start | bytes 589832 | tf_op jit(solution)/shard_map/ppermute | solution.py:17
  107.2 8.0 %collective-permute-start.24 = (bf16[128,768]{1,0:T(8,128)(2,1)S(1)}, bf16[128,768]{1,0:T(8,128)(2,1)S(1)}, u32[]{:S(2)}, u32[]{:S(2)}) collective-permute-start(bf16[128,768]{1,0:T(8,128)(2,1)S(1)} %get-tuple-element.28), channel_id=1, source_target_pairs={{0,64},{64,128},{128,192},{192,0},{1,65},{65,129},{129,193},{193,1... | collective-permute-start | bytes 589832 | tf_op jit(solution)/shard_map/ppermute | solution.py:17
  123.4 20.8 %all-to-all-start = ((bf16[8,32,512]{2,1,0:T(8,128)(2,1)}), bf16[8,32,512]{2,1,0:T(8,128)(2,1)S(1)}, u32[]{:S(2)}, u32[]{:S(2)}) async-start(bf16[8,32,512]{2,1,0:T(8,128)(2,1)} %broadcast_in_dim.68), calls=%async_computation | async-start | bytes 524288 | tf_op jit(solution)/shard_map/all_to_all | solution.py:119
  149.6 9.4 %collective-permute-start.33 = (bf16[64,512]{1,0:T(8,128)(2,1)S(1)}, bf16[64,512]{1,0:T(8,128)(2,1)S(1)}, u32[]{:S(2)}, u32[]{:S(2)}) collective-permute-start(bf16[64,512]{1,0:T(8,128)(2,1)S(1)} %dynamic-slice_bitcast_fusion.4), channel_id=1, source_target_pairs={{0,32},{32,0},{1,33},{33,1},{2,34},{34,2},{3,35},{35,3},{4,36},{36... | collective-permute-start | bytes 196616 | tf_op jit(solution)/shard_map/ppermute | solution.py:133
  (23 other events, 184.8 us)
Sparse Core Ops, SparseCore 0:
  21.1 50.5 all-gather.1
where the time goes:
time: 167 us
  starting transfers between devices  73.3 us (44%)
  waiting for transfers between devices  50 us (30%)
  between operations  14.8 us (9%)
  matrix products  11.2 us (7%)
  other arithmetic  9.54 us (6%)
  local copies, waits for them, and re-layouts  7.73 us (5%)
    ppermute x17, waiting for transfers between devices, shift(): lax.ppermute(array, axis, [(i, (i + by) % size) for i in range(size)])  31.2 us
    ppermute x17, starting transfers between devices, shift(): lax.ppermute(array, axis, [(i, (i + by) % size) for i in range(size)])  22.9 us
    ppermute x2, starting transfers between devices, own_slab_of_both(): got = lax.ppermute(given, 'core', [(0, 1), (1, 0)])  12.6 us
    ppermute x8, starting transfers between devices, from_root(): return lax.ppermute(array, ALL, pairs)  12.1 us
    all_to_all x1, starting transfers between devices, summed_over_col(): part = lax.all_to_all(copies, 'z', split_axis=0, concat_axis=0, tiled=True)  11.4 us
    dot_general x2, matrix products, partial_of(): jnp.einsum('qj,pq->jp', panel, inverse_block, preferred_element_type=F32)  9.75 us
    all_gather x1, waiting for transfers between devices, panel_y_then_z(): return lax.all_gather(part, 'z', axis=0, tiled=True)  8.13 us
    ppermute x1, starting transfers between devices, pair_sum(): lax.ppermute(jnp.where(first, partial[1], partial[0]), 'core', [(0, 1), (...  7.18 us
  transfers between devices with their start and end apart: 36, of which 16 were waited for; matrix products, arithmetic and copies ran while one was open for 13% of the time, Pallas kernels for 0%

commit v1 on v0

--- a/solution.py
+++ b/solution.py
@@ -52,7 +52,9 @@
 
 def panel_y_then_z(piece):
     part = placed_by_owner(direct_ring(piece, "y", YS), lax.axis_index("y"), 0)
-    return lax.all_gather(part, "z", axis=0, tiled=True)
+    return jnp.concatenate(
+        lax.all_to_all(jnp.stack([part] * lax.axis_size("z")), "z", 0, 0), axis=0
+    )
 
 
 def near_z_then_y(piece):

time: 167 us -> 223 us (1.34)
  waiting for transfers between devices: 50 us -> 98.4 us
  starting transfers between devices: 73.3 us -> 92.7 us
  between operations: 14.8 us -> 1.42 us
    ppermute x17, waiting for transfers between devices: 31.2 us -> 89 us  [shift(): lax.ppermute(array, axis, [(i, (i + by) % size) for i in range(size)])]
    all_gather x1 -> x0, waiting for transfers between devices: 8.13 us -> none  [panel_y_then_z(): return lax.all_gather(part, 'z', axis=0, tiled=True)]
    ppermute x1, starting transfers between devices: 7.18 us -> 14.5 us  [pair_sum(): lax.ppermute(jnp.where(first, partial[1], partial[0]), 'core', [(0, 1), (...]
    all_to_all x0 -> x1, starting transfers between devices: none -> 6.38 us  [panel_y_then_z(): lax.all_to_all(jnp.stack([part] * lax.axis_size('z')), 'z', 0, 0)]
    ppermute x17, starting transfers between devices: 22.9 us -> 27.8 us  [shift(): lax.ppermute(array, axis, [(i, (i + by) % size) for i in range(size)])]
  transfers between devices with their start and end apart: 36 -> 36, of which waited for: 16 -> 14; matrix products, arithmetic and copies ran while one was open for 13% -> 10% of each run, Pallas kernels for 0% -> 0%
where the time goes in v1:
time: 223 us; the launch traced here: 222 us
  waiting for transfers between devices  98.4 us (44%)
  starting transfers between devices  92.7 us (42%)
  matrix products  11.3 us (5%)
  other arithmetic  9.49 us (4%)
  local copies, waits for them, and re-layouts  9 us (4%)
    ppermute x17, waiting for transfers between devices, shift(): lax.ppermute(array, axis, [(i, (i + by) % size) for i in range(size)])  89 us
    ppermute x17, starting transfers between devices, shift(): lax.ppermute(array, axis, [(i, (i + by) % size) for i in range(size)])  27.8 us
    ppermute x2, starting transfers between devices, own_slab_of_both(): got = lax.ppermute(given, 'core', [(0, 1), (1, 0)])  14.6 us
    ppermute x1, starting transfers between devices, pair_sum(): lax.ppermute(jnp.where(first, partial[1], partial[0]), 'core', [(0, 1), (...  14.5 us
    ppermute x8, starting transfers between devices, from_root(): return lax.ppermute(array, ALL, pairs)  12.1 us
    dot_general x2, matrix products, partial_of(): jnp.einsum('qj,pq->jp', panel, inverse_block, preferred_element_type=F32)  9.79 us
    all_to_all x1, starting transfers between devices, summed_over_col(): part = lax.all_to_all(copies, 'z', split_axis=0, concat_axis=0, tiled=True)  9.77 us
    ppermute x6, starting transfers between devices, exchanged(): return lax.ppermute(array, axis, [(i, i ^ by) for i in range(size)])  7.57 us
  transfers between devices with their start and end apart: 36, of which 14 were waited for; matrix products, arithmetic and copies ran while one was open for 10% of the time, Pallas kernels for 0%

profile of v1, /device:TPU:1, one launch (start us, length us, event | category | flops | bytes accessed | tf_op | source)
XLA Modules:
  0.0 222.3 jit_solution(16417040624497888058)
XLA Ops:
  3.1 3.8 %collective-permute-start.1 = (bf16[96,512]{1,0:T(8,128)(2,1)S(1)}, bf16[96,512]{1,0:T(8,128)(2,1)S(1)}, u32[]{:S(2)}, u32[]{:S(2)}) collective-permute-start(bf16[96,512]{1,0:T(8,128)(2,1)S(1)} %get-tuple-element.36), channel_id=1, source_target_pairs={{0,2},{1,3},{2,0},{3,1},{4,6},{5,7},{6,4},{7,5},{8,10},{9,11},{10,... | collective-permute-start | bytes 294920 | tf_op jit(solution)/shard_map/ppermute | solution.py:17
  7.4 2.3 %collective-permute-start.2 = (bf16[96,512]{1,0:T(8,128)(2,1)S(1)}, bf16[96,512]{1,0:T(8,128)(2,1)S(1)}, u32[]{:S(2)}, u32[]{:S(2)}) collective-permute-start(bf16[96,512]{1,0:T(8,128)(2,1)S(1)} %get-tuple-element.36), channel_id=1, source_target_pairs={{0,3},{1,0},{2,1},{3,2},{4,7},{5,4},{6,5},{7,6},{8,11},{9,8},{10,9... | collective-permute-start | bytes 294920 | tf_op jit(solution)/shard_map/ppermute | solution.py:17
  9.8 3.8 %collective-permute-done = bf16[96,512]{1,0:T(8,128)(2,1)S(1)} collective-permute-done((bf16[96,512]{1,0:T(8,128)(2,1)S(1)}, bf16[96,512]{1,0:T(8,128)(2,1)S(1)}, u32[]{:S(2)}, u32[]{:S(2)}) %collective-permute-start) | collective-permute-done | bytes 98336 | tf_op jit(solution)/shard_map/ppermute | solution.py:17
  15.6 6.4 %all-to-all-start = ((bf16[8,384,512]{2,1,0:T(8,128)(2,1)}), bf16[8,384,512]{2,1,0:T(8,128)(2,1)}, u32[]{:S(2)}, u32[]{:S(2)}) async-start(bf16[8,384,512]{2,1,0:T(8,128)(2,1)} %stack.14), calls=%async_computation | async-start | bytes 6291456 | tf_op jit(solution)/shard_map/all_to_all | solution.py:56
  25.0 60.5 %collective-permute-done.3 = bf16[1,96,512]{2,1,0:T(8,128)(2,1)S(1)} collective-permute-done((bf16[1,96,512]{2,1,0:T(8,128)(2,1)S(1)}, bf16[1,96,512]{2,1,0:T(8,128)(2,1)S(1)}, u32[]{:S(2)}, u32[]{:S(2)}) %collective-permute-start.3) | collective-permute-done | bytes 98336 | tf_op jit(solution)/shard_map/ppermute | solution.py:17
  85.5 6.4 %collective-permute-start.4 = (bf16[1,96,512]{2,1,0:T(8,128)(2,1)S(1)}, bf16[1,96,512]{2,1,0:T(8,128)(2,1)S(1)}, u32[]{:S(2)}, u32[]{:S(2)}) collective-permute-start(bf16[1,96,512]{2,1,0:T(8,128)(2,1)S(1)} %collective-permute-done.3), channel_id=1, source_target_pairs={{0,4},{4,8},{8,12},{12,16},{16,20},{20,24},{24,28},{28,0},{1,5},{5... | collective-permute-start | bytes 294920 | tf_op jit(solution)/shard_map/ppermute | solution.py:17
  91.9 2.9 %collective-permute-start.8 = (bf16[1,96,512]{2,1,0:T(8,128)(2,1)S(1)}, bf16[1,96,512]{2,1,0:T(8,128)(2,1)S(1)}, u32[]{:S(2)}, u32[]{:S(2)}) collective-permute-start(bf16[1,96,512]{2,1,0:T(8,128)(2,1)S(1)} %collective-permute-done.7), channel_id=1, source_target_pairs={{0,28},{4,0},{8,4},{12,8},{16,12},{20,16},{24,20},{28,24},{1,29},{... | collective-permute-start | bytes 294920 | tf_op jit(solution)/shard_map/ppermute | solution.py:17
  96.9 2.7 %collective-permute-start.9 = (bf16[1,96,512]{2,1,0:T(8,128)(2,1)S(1)}, bf16[1,96,512]{2,1,0:T(8,128)(2,1)S(1)}, u32[]{:S(2)}, u32[]{:S(2)}) collective-permute-start(bf16[1,96,512]{2,1,0:T(8,128)(2,1)S(1)} %collective-permute-done.8), channel_id=1, source_target_pairs={{0,28},{4,0},{8,4},{12,8},{16,12},{20,16},{24,20},{28,24},{1,29},{... | collective-permute-start | bytes 294920 | tf_op jit(solution)/shard_map/ppermute | solution.py:17
  101.6 5.5 %collective-permute-done.6 = bf16[1,96,512]{2,1,0:T(8,128)(2,1)S(1)} collective-permute-done((bf16[1,96,512]{2,1,0:T(8,128)(2,1)S(1)}, bf16[1,96,512]{2,1,0:T(8,128)(2,1)S(1)}, u32[]{:S(2)}, u32[]{:S(2)}) %collective-permute-start.6) | collective-permute-done | bytes 98336 | tf_op jit(solution)/shard_map/ppermute | solution.py:17
  107.1 2.5 %collective-permute-start.10 = (bf16[8,1,96,512]{3,2,1,0:T(8,128)(2,1)S(1)}, bf16[8,1,96,512]{3,2,1,0:T(8,128)(2,1)}, u32[]{:S(2)}, u32[]{:S(2)}) collective-permute-start(bf16[8,1,96,512]{3,2,1,0:T(8,128)(2,1)S(1)} %bitcast_dynamic-update-slice_fusion), channel_id=1, source_target_pairs={{0,1},{1,2},{2,3},{3,0},{4,5},{5,6},{6,7},{7,4},{8,9},{9,10},{10,1... | collective-permute-start | bytes 2359304 | tf_op jit(solution)/shard_map/ppermute | solution.py:17
  112.1 8.7 %collective-permute-done.10 = bf16[8,1,96,512]{3,2,1,0:T(8,128)(2,1)} collective-permute-done((bf16[8,1,96,512]{3,2,1,0:T(8,128)(2,1)S(1)}, bf16[8,1,96,512]{3,2,1,0:T(8,128)(2,1)}, u32[]{:S(2)}, u32[]{:S(2)}) %collective-permute-start.10) | collective-permute-done | bytes 786464 | tf_op jit(solution)/shard_map/ppermute | solution.py:17
  130.7 5.9 %convolution_convert_fusion.1 = bf16[512,768]{1,0:T(8,128)(2,1)S(1)} fusion(bf16[3072,512]{1,0:T(8,128)(2,1)} %bitcast.1, bf16[768,3072]{1,0:T(8,128)(2,1)} %param.8), kind=kOutput, calls=%fused_computation.2 | convolution fusion | flops 2416312320 | bytes 8650752 | tf_op jit(solution)/shard_map/qj,pq->jp/dot_general | solution.py:156
  136.7 2.6 %broadcast_select_fusion = (bf16[768,512]{1,0:T(8,128)(2,1)}, bf16[768,512]{1,0:T(8,128)(2,1)S(1)}) fusion(pred[]{:T(512)S(6)} %eq.63, bf16[2,4,96,512]{3,2,1,0:T(8,128)(2,1)S(1)} %dynamic-slice_dynamic-update-slice_fusion, bf16[3072,512]{1,0:T(8,128)(2,1)} %bitcast.1, s32[]{:T(128)S(6)} %select_n.299), kind=kLoop, calls=%fused_computation.9 | loop fusion | flops 393216 | bytes 3145733 | tf_op jit(solution)/shard_map/jit(_where)/select_n | solution.py:175
  147.2 3.8 %broadcast_select_fusion.1 = (bf16[512,768]{1,0:T(8,128)(2,1)}, bf16[512,768]{1,0:T(8,128)(2,1)}) fusion(bf16[512,768]{1,0:T(8,128)(2,1)S(1)} %convolution_convert_fusion.1, pred[]{:T(512)S(6)} %eq.63, bf16[3072,512]{1,0:T(8,128)(2,1)S(1)} %bitcast.97, bf16[768,3072]{1,0:T(8,128)(2,1)S(1)} %bitcast.109), kind=kOutput, calls=%fused_computation.10 | convolution fusion | flops 2416705536 | bytes 10223617 | tf_op jit(solution)/shard_map/qj,pq->jp/dot_general | solution.py:156
  151.1 14.5 %collective-permute-start.14 = (bf16[512,768]{1,0:T(8,128)(2,1)}, bf16[512,768]{1,0:T(8,128)(2,1)}, u32[]{:S(2)}, u32[]{:S(2)}) collective-permute-start(bf16[512,768]{1,0:T(8,128)(2,1)} %get-tuple-element.40), channel_id=1, source_target_pairs={{0,32},{32,0},{1,33},{33,1},{2,34},{34,2},{3,35},{35,3},{4,36},{36... | collective-permute-start | bytes 2359304 | tf_op jit(solution)/shard_map/ppermute | solution.py:94
  165.6 2.7 %add_select_fusion = bf16[768,512]{1,0:T(8,128)(2,1)S(1)} fusion(bf16[768,512]{1,0:T(8,128)(2,1)S(1)} %collective-permute-done.22, bf16[768,512]{1,0:T(8,128)(2,1)} %collective-permute-done.21, bf16[768,512]{1,0:T(8,128)(2,1)} %collective-permute-done.19, bf16[768,512]{1,0:T(8,128)(2,1)} %collective-permute-done.20, ...), kind=kLoop, calls=%fused_computation.8 | loop fusion | flops 3145728 | bytes 7864322 | tf_op jit(solution)/shard_map/jit(_where)/select_n | solution.py:178
  171.7 4.4 %collective-permute-done.23 = bf16[128,768]{1,0:T(8,128)(2,1)S(1)} collective-permute-done((bf16[128,768]{1,0:T(8,128)(2,1)S(1)}, bf16[128,768]{1,0:T(8,128)(2,1)S(1)}, u32[]{:S(2)}, u32[]{:S(2)}) %collective-permute-start.23) | collective-permute-done | bytes 196640 | tf_op jit(solution)/shard_map/ppermute | solution.py:17
  178.9 2.9 %collective-permute-start.29 = (bf16[32,512]{1,0:T(8,128)(2,1)S(1)}, bf16[32,512]{1,0:T(8,128)(2,1)S(1)}, u32[]{:S(2)}, u32[]{:S(2)}) collective-permute-start(bf16[32,512]{1,0:T(8,128)(2,1)S(1)} %get-tuple-element.38), channel_id=1, source_target_pairs={{0,3},{1,2},{2,1},{3,0},{4,7},{5,6},{6,5},{7,4},{8,11},{9,10},{10,... | collective-permute-start | bytes 98312 | tf_op jit(solution)/shard_map/ppermute | solution.py:109
  183.0 3.0 %collective-permute-done.28 = bf16[32,512]{1,0:T(8,128)(2,1)S(1)} collective-permute-done((bf16[32,512]{1,0:T(8,128)(2,1)S(1)}, bf16[32,512]{1,0:T(8,128)(2,1)S(1)}, u32[]{:S(2)}, u32[]{:S(2)}) %collective-permute-start.28) | collective-permute-done | bytes 32800 | tf_op jit(solution)/shard_map/ppermute | solution.py:109
  186.7 9.8 %all-to-all-start.1 = ((bf16[8,32,512]{2,1,0:T(8,128)(2,1)}), bf16[8,32,512]{2,1,0:T(8,128)(2,1)S(1)}, u32[]{:S(2)}, u32[]{:S(2)}) async-start(bf16[8,32,512]{2,1,0:T(8,128)(2,1)} %broadcast_in_dim.65), calls=%async_computation.1 | async-start | bytes 524288 | tf_op jit(solution)/shard_map/all_to_all | solution.py:121
  196.5 5.6 %collective-permute-start.26 = (bf16[64,768]{1,0:T(8,128)(2,1)S(1)}, bf16[64,768]{1,0:T(8,128)(2,1)S(1)}, u32[]{:S(2)}, u32[]{:S(2)}) collective-permute-start(bf16[64,768]{1,0:T(8,128)(2,1)S(1)} %dynamic-slice_bitcast_fusion.3), channel_id=1, source_target_pairs={{0,32},{32,0},{1,33},{33,1},{2,34},{34,2},{3,35},{35,3},{4,36},{36... | collective-permute-start | bytes 294920 | tf_op jit(solution)/shard_map/ppermute | solution.py:135
  203.1 2.7 %all-to-all-done.1 = bf16[8,32,512]{2,1,0:T(8,128)(2,1)S(1)} async-done(((bf16[8,32,512]{2,1,0:T(8,128)(2,1)}), bf16[8,32,512]{2,1,0:T(8,128)(2,1)S(1)}, u32[]{:S(2)}, u32[]{:S(2)}) %all-to-all-start.1) | async-done | bytes 262176 | tf_op jit(solution)/shard_map/all_to_all | solution.py:121
  209.3 2.3 %collective-permute-done.30 = bf16[32,512]{1,0:T(8,128)(2,1)S(1)} collective-permute-done((bf16[32,512]{1,0:T(8,128)(2,1)S(1)}, bf16[32,512]{1,0:T(8,128)(2,1)S(1)}, u32[]{:S(2)}, u32[]{:S(2)}) %collective-permute-start.30) | collective-permute-done | bytes 32800 | tf_op jit(solution)/shard_map/ppermute | solution.py:109
  211.6 9.0 %collective-permute-start.33 = (bf16[64,512]{1,0:T(8,128)(2,1)S(1)}, bf16[64,512]{1,0:T(8,128)(2,1)S(1)}, u32[]{:S(2)}, u32[]{:S(2)}) collective-permute-start(bf16[64,512]{1,0:T(8,128)(2,1)S(1)} %dynamic-slice_bitcast_fusion.4), channel_id=1, source_target_pairs={{0,32},{32,0},{1,33},{33,1},{2,34},{34,2},{3,35},{35,3},{4,36},{36... | collective-permute-start | bytes 196616 | tf_op jit(solution)/shard_map/ppermute | solution.py:135
  (128 shorter events, 46.1 us)
Async XLA Ops:
  3.1 10.5 %collective-permute-start.1 = (bf16[96,512]{1,0:T(8,128)(2,1)S(1)}, bf16[96,512]{1,0:T(8,128)(2,1)S(1)}, u32[]{:S(2)}, u32[]{:S(2)}) collective-permute-start(bf16[96,512]{1,0:T(8,128)(2,1)S(1)} %get-tuple-element.36), channel_id=1, source_target_pairs={{0,2},{1,3},{2,0},{3,1},{4,6},{5,7},{6,4},{7,5},{8,10},{9,11},{10,... | collective-permute-start | bytes 294920 | tf_op jit(solution)/shard_map/ppermute | solution.py:17
  7.0 6.6 %collective-permute-start = (bf16[96,512]{1,0:T(8,128)(2,1)S(1)}, bf16[96,512]{1,0:T(8,128)(2,1)S(1)}, u32[]{:S(2)}, u32[]{:S(2)}) collective-permute-start(bf16[96,512]{1,0:T(8,128)(2,1)S(1)} %get-tuple-element.36), channel_id=1, source_target_pairs={{0,1},{1,2},{2,3},{3,0},{4,5},{5,6},{6,7},{7,4},{8,9},{9,10},{10,1... | collective-permute-start | bytes 294920 | tf_op jit(solution)/shard_map/ppermute | solution.py:17
  15.6 111.9 %all-to-all-start = ((bf16[8,384,512]{2,1,0:T(8,128)(2,1)}), bf16[8,384,512]{2,1,0:T(8,128)(2,1)}, u32[]{:S(2)}, u32[]{:S(2)}) async-start(bf16[8,384,512]{2,1,0:T(8,128)(2,1)} %stack.14), calls=%async_computation | async-start | bytes 6291456 | tf_op jit(solution)/shard_map/all_to_all | solution.py:56
  22.0 63.5 %collective-permute-start.3 = (bf16[1,96,512]{2,1,0:T(8,128)(2,1)S(1)}, bf16[1,96,512]{2,1,0:T(8,128)(2,1)S(1)}, u32[]{:S(2)}, u32[]{:S(2)}) collective-permute-start(bf16[1,96,512]{2,1,0:T(8,128)(2,1)S(1)} %get-tuple-element.35), channel_id=1, source_target_pairs={{0,4},{4,8},{8,12},{12,16},{16,20},{20,24},{24,28},{28,0},{1,5},{5... | collective-permute-start | bytes 294920 | tf_op jit(solution)/shard_map/ppermute | solution.py:17
  23.5 68.4 %collective-permute-start.7 = (bf16[1,96,512]{2,1,0:T(8,128)(2,1)S(1)}, bf16[1,96,512]{2,1,0:T(8,128)(2,1)S(1)}, u32[]{:S(2)}, u32[]{:S(2)}) collective-permute-start(bf16[1,96,512]{2,1,0:T(8,128)(2,1)S(1)} %get-tuple-element.35), channel_id=1, source_target_pairs={{0,28},{4,0},{8,4},{12,8},{16,12},{20,16},{24,20},{28,24},{1,29},{... | collective-permute-start | bytes 294920 | tf_op jit(solution)/shard_map/ppermute | solution.py:17
  85.5 11.4 %collective-permute-start.4 = (bf16[1,96,512]{2,1,0:T(8,128)(2,1)S(1)}, bf16[1,96,512]{2,1,0:T(8,128)(2,1)S(1)}, u32[]{:S(2)}, u32[]{:S(2)}) collective-permute-start(bf16[1,96,512]{2,1,0:T(8,128)(2,1)S(1)} %collective-permute-done.3), channel_id=1, source_target_pairs={{0,4},{4,8},{8,12},{12,16},{16,20},{20,24},{24,28},{28,0},{1,5},{5... | collective-permute-start | bytes 294920 | tf_op jit(solution)/shard_map/ppermute | solution.py:17
  96.9 10.2 %collective-permute-start.9 = (bf16[1,96,512]{2,1,0:T(8,128)(2,1)S(1)}, bf16[1,96,512]{2,1,0:T(8,128)(2,1)S(1)}, u32[]{:S(2)}, u32[]{:S(2)}) collective-permute-start(bf16[1,96,512]{2,1,0:T(8,128)(2,1)S(1)} %collective-permute-done.8), channel_id=1, source_target_pairs={{0,28},{4,0},{8,4},{12,8},{16,12},{20,16},{24,20},{28,24},{1,29},{... | collective-permute-start | bytes 294920 | tf_op jit(solution)/shard_map/ppermute | solution.py:17
  107.1 13.7 %collective-permute-start.10 = (bf16[8,1,96,512]{3,2,1,0:T(8,128)(2,1)S(1)}, bf16[8,1,96,512]{3,2,1,0:T(8,128)(2,1)}, u32[]{:S(2)}, u32[]{:S(2)}) collective-permute-start(bf16[8,1,96,512]{3,2,1,0:T(8,128)(2,1)S(1)} %bitcast_dynamic-update-slice_fusion), channel_id=1, source_target_pairs={{0,1},{1,2},{2,3},{3,0},{4,5},{5,6},{6,7},{7,4},{8,9},{9,10},{10,1... | collective-permute-start | bytes 2359304 | tf_op jit(solution)/shard_map/ppermute | solution.py:17
  109.6 13.1 %collective-permute-start.11 = (bf16[8,1,96,512]{3,2,1,0:T(8,128)(2,1)S(1)}, bf16[8,1,96,512]{3,2,1,0:T(8,128)(2,1)S(1)}, u32[]{:S(2)}, u32[]{:S(2)}) collective-permute-start(bf16[8,1,96,512]{3,2,1,0:T(8,128)(2,1)S(1)} %bitcast_dynamic-update-slice_fusion), channel_id=1, source_target_pairs={{0,3},{1,0},{2,1},{3,2},{4,7},{5,4},{6,5},{7,6},{8,11},{9,8},{10,9... | collective-permute-start | bytes 2359304 | tf_op jit(solution)/shard_map/ppermute | solution.py:17
  110.8 11.0 %collective-permute-start.15 = (bf16[2,1,96,512]{3,2,1,0:T(8,128)(2,1)}, bf16[2,1,96,512]{3,2,1,0:T(8,128)(2,1)}, u32[]{:S(2)}, u32[]{:S(2)}) collective-permute-start(bf16[2,1,96,512]{3,2,1,0:T(8,128)(2,1)} %get-tuple-element.29), channel_id=1, source_target_pairs={{0,2},{1,3},{2,0},{3,1},{36,38},{37,39},{38,36},{39,37},{72,74},{7... | collective-permute-start | bytes 589832 | tf_op jit(solution)/shard_map/ppermute | solution.py:85
  122.8 21.6 %collective-permute-start.20 = (bf16[768,512]{1,0:T(8,128)(2,1)S(1)}, bf16[768,512]{1,0:T(8,128)(2,1)}, u32[]{:S(2)}, u32[]{:S(2)}) collective-permute-start(bf16[768,512]{1,0:T(8,128)(2,1)S(1)} %bitcast.94), channel_id=1, source_target_pairs={{0,224},{1,225},{2,226},{3,227},{36,228},{37,229},{38,230},{39,231... | collective-permute-start | bytes 2359304 | tf_op jit(solution)/shard_map/ppermute | solution.py:85
  124.4 21.5 %collective-permute-start.19 = (bf16[768,512]{1,0:T(8,128)(2,1)S(1)}, bf16[768,512]{1,0:T(8,128)(2,1)}, u32[]{:S(2)}, u32[]{:S(2)}) collective-permute-start(bf16[768,512]{1,0:T(8,128)(2,1)S(1)} %bitcast.95), channel_id=1, source_target_pairs={{0,96},{1,97},{2,98},{3,99},{36,100},{37,101},{38,102},{39,103},{7... | collective-permute-start | bytes 2359304 | tf_op jit(solution)/shard_map/ppermute | solution.py:85
  126.0 25.1 %collective-permute-start.21 = (bf16[768,512]{1,0:T(8,128)(2,1)S(1)}, bf16[768,512]{1,0:T(8,128)(2,1)}, u32[]{:S(2)}, u32[]{:S(2)}) collective-permute-start(bf16[768,512]{1,0:T(8,128)(2,1)S(1)} %bitcast.96), channel_id=1, source_target_pairs={{0,160},{1,161},{2,162},{3,163},{36,164},{37,165},{38,166},{39,167... | collective-permute-start | bytes 2359304 | tf_op jit(solution)/shard_map/ppermute | solution.py:85
  128.6 10.7 %collective-permute-start.13 = (bf16[4,1,96,512]{3,2,1,0:T(8,128)(2,1)S(1)}, bf16[4,1,96,512]{3,2,1,0:T(8,128)(2,1)S(1)}, u32[]{:S(2)}, u32[]{:S(2)}) collective-permute-start(bf16[4,1,96,512]{3,2,1,0:T(8,128)(2,1)S(1)} %slice.19), channel_id=1, source_target_pairs={{0,3},{1,0},{2,1},{3,2},{4,7},{5,4},{6,5},{7,6},{8,11},{9,8},{10,9... | collective-permute-start | bytes 1179656 | tf_op jit(solution)/shard_map/ppermute | solution.py:17
  129.9 11.0 %collective-permute-start.12 = (bf16[4,1,96,512]{3,2,1,0:T(8,128)(2,1)S(1)}, bf16[4,1,96,512]{3,2,1,0:T(8,128)(2,1)S(1)}, u32[]{:S(2)}, u32[]{:S(2)}) collective-permute-start(bf16[4,1,96,512]{3,2,1,0:T(8,128)(2,1)S(1)} %slice.18), channel_id=1, source_target_pairs={{0,1},{1,2},{2,3},{3,0},{4,5},{5,6},{6,7},{7,4},{8,9},{9,10},{10,1... | collective-permute-start | bytes 1179656 | tf_op jit(solution)/shard_map/ppermute | solution.py:17
  139.3 26.4 %collective-permute-start.18 = (bf16[768,512]{1,0:T(8,128)(2,1)S(1)}, bf16[768,512]{1,0:T(8,128)(2,1)}, u32[]{:S(2)}, u32[]{:S(2)}) collective-permute-start(bf16[768,512]{1,0:T(8,128)(2,1)S(1)} %get-tuple-element.25), channel_id=1, source_target_pairs={{0,128},{1,129},{2,130},{3,131},{36,132},{37,133},{38,134},{39,135... | collective-permute-start | bytes 2359304 | tf_op jit(solution)/shard_map/ppermute | solution.py:85
  140.8 24.8 %collective-permute-start.17 = (bf16[768,512]{1,0:T(8,128)(2,1)S(1)}, bf16[768,512]{1,0:T(8,128)(2,1)}, u32[]{:S(2)}, u32[]{:S(2)}) collective-permute-start(bf16[768,512]{1,0:T(8,128)(2,1)S(1)} %get-tuple-element.25), channel_id=1, source_target_pairs={{0,192},{1,193},{2,194},{3,195},{36,196},{37,197},{38,198},{39,199... | collective-permute-start | bytes 2359304 | tf_op jit(solution)/shard_map/ppermute | solution.py:85
  144.3 21.3 %collective-permute-start.16 = (bf16[768,512]{1,0:T(8,128)(2,1)S(1)}, bf16[768,512]{1,0:T(8,128)(2,1)}, u32[]{:S(2)}, u32[]{:S(2)}) collective-permute-start(bf16[768,512]{1,0:T(8,128)(2,1)S(1)} %get-tuple-element.25), channel_id=1, source_target_pairs={{0,64},{1,65},{2,66},{3,67},{36,68},{37,69},{38,70},{39,71},{72,13... | collective-permute-start | bytes 2359304 | tf_op jit(solution)/shard_map/ppermute | solution.py:85
  145.9 19.7 %collective-permute-start.22 = (bf16[768,512]{1,0:T(8,128)(2,1)}, bf16[768,512]{1,0:T(8,128)(2,1)S(1)}, u32[]{:S(2)}, u32[]{:S(2)}) collective-permute-start(bf16[768,512]{1,0:T(8,128)(2,1)} %get-tuple-element.24), channel_id=1, source_target_pairs={{0,32},{1,33},{2,34},{3,35},{36,4},{37,5},{38,6},{39,7},{72,104},{... | collective-permute-start | bytes 2359304 | tf_op jit(solution)/shard_map/ppermute | solution.py:85
  151.1 17.3 %collective-permute-start.14 = (bf16[512,768]{1,0:T(8,128)(2,1)}, bf16[512,768]{1,0:T(8,128)(2,1)}, u32[]{:S(2)}, u32[]{:S(2)}) collective-permute-start(bf16[512,768]{1,0:T(8,128)(2,1)} %get-tuple-element.40), channel_id=1, source_target_pairs={{0,32},{32,0},{1,33},{33,1},{2,34},{34,2},{3,35},{35,3},{4,36},{36... | collective-permute-start | bytes 2359304 | tf_op jit(solution)/shard_map/ppermute | solution.py:94
  170.1 8.0 %collective-permute-start.24 = (bf16[128,768]{1,0:T(8,128)(2,1)S(1)}, bf16[128,768]{1,0:T(8,128)(2,1)S(1)}, u32[]{:S(2)}, u32[]{:S(2)}) collective-permute-start(bf16[128,768]{1,0:T(8,128)(2,1)S(1)} %get-tuple-element.28), channel_id=1, source_target_pairs={{0,64},{64,128},{128,192},{192,0},{1,65},{65,129},{129,193},{193,1... | collective-permute-start | bytes 589832 | tf_op jit(solution)/shard_map/ppermute | solution.py:17
  186.7 19.1 %all-to-all-start.1 = ((bf16[8,32,512]{2,1,0:T(8,128)(2,1)}), bf16[8,32,512]{2,1,0:T(8,128)(2,1)S(1)}, u32[]{:S(2)}, u32[]{:S(2)}) async-start(bf16[8,32,512]{2,1,0:T(8,128)(2,1)} %broadcast_in_dim.65), calls=%async_computation.1 | async-start | bytes 524288 | tf_op jit(solution)/shard_map/all_to_all | solution.py:121
  196.5 6.6 %collective-permute-start.26 = (bf16[64,768]{1,0:T(8,128)(2,1)S(1)}, bf16[64,768]{1,0:T(8,128)(2,1)S(1)}, u32[]{:S(2)}, u32[]{:S(2)}) collective-permute-start(bf16[64,768]{1,0:T(8,128)(2,1)S(1)} %dynamic-slice_bitcast_fusion.3), channel_id=1, source_target_pairs={{0,32},{32,0},{1,33},{33,1},{2,34},{34,2},{3,35},{35,3},{4,36},{36... | collective-permute-start | bytes 294920 | tf_op jit(solution)/shard_map/ppermute | solution.py:135
  211.6 9.9 %collective-permute-start.33 = (bf16[64,512]{1,0:T(8,128)(2,1)S(1)}, bf16[64,512]{1,0:T(8,128)(2,1)S(1)}, u32[]{:S(2)}, u32[]{:S(2)}) collective-permute-start(bf16[64,512]{1,0:T(8,128)(2,1)S(1)} %dynamic-slice_bitcast_fusion.4), channel_id=1, source_target_pairs={{0,32},{32,0},{1,33},{33,1},{2,34},{34,2},{3,35},{35,3},{4,36},{36... | collective-permute-start | bytes 196616 | tf_op jit(solution)/shard_map/ppermute | solution.py:135
  (22 other events, 179.2 us)
